TPU v7x, 32 devices: a whole 2x2x4 slice. The times are simulated.
32 devices in a mesh: bond: 8 (over z, x), mpo: 4 (over y, core).
Axes of the slice: x: 2, y: 2, z: 4, core: 2. Of those that a mesh axis runs over, the one named last changes fastest.
Arguments:
- wave_blocks: bfloat16 [8, 16, 256, 256], P('bond'), may hold values from -6 to 6
- left_environment: bfloat16 [8, 8, 256, 256], P('mpo', 'bond'), may hold values from -0.375 to 0.375
- right_environment: bfloat16 [8, 8, 256, 256], P('mpo', 'bond'), may hold values from -0.375 to 0.375
- site_operators: bfloat16 [8, 16, 16], P('mpo'), may hold values from -1.1953125 to 1.1953125
- right_sector: int32 [8, 16, 1], P('bond'), may hold values from 0 to 7; in each aligned block of 16 rows (0 to 15, 16 to 31, ..., all dimensions but the last counted through in order) at most 2 rows name the same one
- left_sizes: int32 [8], replicated, may hold values from 128 to 256
- right_sizes: int32 [8], replicated, may hold values from 128 to 256
- sector_place: int32 [8], replicated, may hold values from 0 to 7, each once
Outputs:
- applied: bfloat16 [8, 16, 256, 256], P('bond', 'mpo')
Inputs may be any that keep to these rules, and one draw needn't show every extreme that they name: `right_sector`: among the 16 blocks of one bond index no right sector is named more than 2 times, a bound that some block reaches. `sector_place`: every position is taken by exactly one right sector.
All inputs are finite; a program needn't handle non-finite values.
Results may differ from a plain program's by a relative error of at most 0.0057.
Values may be sent and summed in bfloat16 or wider, within the bound.
A program may use at most 64 MiB of HBM per device.

v0:
```python
import jax
import jax.numpy as jnp
from jax import lax
from jax.sharding import PartitionSpec as P


def lookup(entries, indices):
    count = entries.shape[0]
    matches = indices[..., None] == jnp.arange(count, dtype=jnp.int32)
    return jnp.sum(jnp.where(matches, entries, 0), axis=-1)


def shards(
    wave_blocks,
    left_environment,
    right_environment,
    site_operators,
    right_sector,
    left_sizes,
    right_sizes,
    sector_place,
):
    sectors = wave_blocks.shape[0]
    states = wave_blocks.shape[1]
    block_rows = wave_blocks.shape[2]
    channels = left_environment.shape[0]
    first_sector = lax.axis_index("bond") * sectors
    sector_ids = right_sector[:, :, 0]
    offsets = jnp.arange(block_rows, dtype=jnp.int32)
    left_live = lax.dynamic_slice_in_dim(left_sizes, first_sector, sectors)
    row_mask = offsets[None, :] < left_live[:, None]
    column_mask = offsets[None, None, :] < lookup(right_sizes, sector_ids)[:, :, None]
    live_mask = row_mask[:, None, :, None] & column_mask[:, :, None, :]
    masked = jnp.where(live_mask, wave_blocks, jnp.zeros((), jnp.bfloat16))
    block_count = sectors * states
    flat_blocks = masked.reshape(block_count, block_rows, block_rows)
    place_flat = lookup(sector_place, sector_ids).reshape(block_count)
    gathered = lax.all_gather(right_environment, "bond", axis=1, tiled=True)
    chosen = jnp.take(gathered, place_flat, axis=1)
    right_part = jnp.einsum(
        "bac,hbxc->bhax", flat_blocks, chosen, preferred_element_type=jnp.float32
    ).astype(jnp.bfloat16)
    right_part = right_part.reshape(sectors, states, channels, block_rows, block_rows)
    same_sector = sector_ids[:, :, None] == sector_ids[:, None, :]
    mixing = jnp.where(same_sector[:, None], site_operators[None], jnp.zeros((), jnp.bfloat16))
    mixed = jnp.einsum(
        "nhst,nthac->nshac", mixing, right_part, preferred_element_type=jnp.float32
    ).astype(jnp.bfloat16)
    partial_value = jnp.einsum(
        "hnab,nshbc->nsac", left_environment, mixed, preferred_element_type=jnp.float32
    )
    per_device = states // lax.axis_size("mpo")
    first_state = lax.axis_index("mpo") * per_device
    summed = lax.psum(partial_value, "mpo")
    summed = lax.dynamic_slice_in_dim(summed, first_state, per_device, 1)
    kept_mask = lax.dynamic_slice_in_dim(live_mask, first_state, per_device, 1)
    return jnp.where(kept_mask, summed, jnp.zeros((), jnp.float32)).astype(jnp.bfloat16)


def solution(mesh):
    placed = (
        P("bond", None, None, None),
        P("mpo", "bond", None, None),
        P("mpo", "bond", None, None),
        P("mpo", None, None),
        P("bond", None, None),
        P(),
        P(),
        P(),
    )
    return jax.shard_map(
        shards, mesh=mesh, in_specs=placed, out_specs=P("bond", "mpo", None, None), check_vma=False
    )
```

profile of v0, /device:TPU:0, one launch (start us, length us, event | category | flops | bytes accessed | tf_op | source)
XLA Modules:
  0.0 172.7 jit_solution(5104987714782508854)
XLA Ops:
  6.5 0.0 copy-start
  6.5 0.0 copy-start.5
  6.5 0.0 copy-start.2
  6.5 0.0 copy-start.3
  6.5 0.0 copy-start.4
  6.5 0.0 all-gather.2.cloned.1.call-start
  6.6 0.7 all-gather.2.cloned.1.call-update
  7.3 2.9 %copy.12 = bf16[1,16,256,256]{2,3,1,0:T(8,128)(2,1)S(1)} copy(bf16[1,16,256,256]{3,2,1,0:T(8,128)(2,1)} %param.8) | data formatting | bytes 4194304 | tf_op args[0]
  10.2 0.0 copy-done.5
  10.2 0.6 dynamic_slice.9
  10.8 0.6 iota_compare_fusion.2
  11.4 0.0 copy-done.2
  11.4 0.0 copy-done.3
  11.4 0.0 copy-done.4
  11.4 0.1 select_reduce_fusion.1
  11.6 0.1 broadcast_compare_fusion
  11.6 0.1 iota_compare_fusion
  11.7 2.0 %broadcast_and_fusion = pred[1,16,256,256]{2,3,1,0:T(8,128)(4,1)} fusion(pred[16,256]{1,0:T(8,128)(4,1)S(1)} %iota_compare_fusion, pred[256]{0:T(512)(128)(4,1)S(1)} %iota_compare_fusion.2), kind=kLoop, calls=%fused_computation.15 | loop fusion | flops 1048576 | bytes 1052928 | tf_op jit(solution)/shard_map/and | solution.py:33
  13.7 47.6 %all-gather.2.cloned.1.call-done = bf16[2,8,256,256]{3,2,1,0:T(8,128)(2,1)} async-done(((bf16[2,1,256,256]{3,2,1,0:T(8,128)(2,1)}), bf16[2,8,256,256]{3,2,1,0:T(8,128)(2,1)}) %all-gather.2.cloned.1.call-update) | async-done | bytes 2097168 | tf_op jit(solution)/shard_map/all_gather | solution.py:38
  61.4 4.3 %gather_fusion = bf16[16,2,256,256]{3,2,1,0:T(8,128)(2,1)} fusion(bf16[2,8,256,256]{3,2,1,0:T(8,128)(2,1)} %all-gather.2.cloned.1.call-done, s32[1024]{0:T(1024)S(1)} %pad_clamp_fusion), kind=kCustom, calls=%fused_computation | custom fusion | bytes 8388672 | tf_op jit(solution)/shard_map/jit(_take)/gather | solution.py:39
  65.7 4.7 %fusion.2 = bf16[16,2,256,256]{3,2,1,0:T(8,128)(2,1)} fusion(bf16[16,2,256,256]{3,2,1,0:T(8,128)(2,1)} %gather_fusion, pred[16]{0:T(512)(128)(4,1)S(1)} %compare_and_fusion, bf16[1,16,256,256]{2,3,1,0:T(8,128)(2,1)S(1)} %copy.12, pred[16,256]{1,0:T(8,128)(4,1)S(1)} %iota_compare_fusion, pred[256]{0:T(512)(128)(4,1)S(1)} %iota_compare_fusion.2), kind=kOutput, calls=%fused_computation.3 | convolution fusion | flops 1077936128 | bytes 10490128 | tf_op jit(solution)/shard_map/bac,hbxc->bhax/dot_general | solution.py:40
  70.4 0.0 copy-start.1
  70.4 7.9 %copy.16 = bf16[16,2,256,256]{2,0,3,1:T(8,128)(2,1)} copy(bf16[16,2,256,256]{3,2,1,0:T(8,128)(2,1)} %fusion.2) | data formatting | bytes 8388608 | tf_op jit(solution)/shard_map/bac,hbxc->bhax/dot_general | solution.py:40
  78.3 0.0 copy-done.1
  78.3 3.4 %convert_bitcast_fusion = bf16[16,2,256,256]{3,0,2,1:T(8,128)(2,1)S(1)} fusion(bf16[16,2,256,256]{2,0,3,1:T(8,128)(2,1)} %copy.16, bf16[2,16,16]{2,1,0:T(8,128)(2,1)S(1)} %copy-done.1, pred[16,16]{1,0:T(8,128)(4,1)S(1)} %broadcast_compare_fusion), kind=kOutput, calls=%fused_computation.8 | convolution fusion | flops 69206528 | bytes 8389888 | tf_op jit(solution)/shard_map/nhst,nthac->nshac/dot_general | solution.py:46
  81.7 0.0 copy-done
  81.7 6.1 %fusion.11 = f32[1,16,256,256]{2,3,1,0:T(8,128)} fusion(bf16[16,2,256,256]{3,0,2,1:T(8,128)(2,1)S(1)} %convert_bitcast_fusion, bf16[2,1,256,256]{3,2,1,0:T(8,128)(2,1)S(1)} %copy-done), kind=kOutput, calls=%fused_computation.11 | convolution fusion | flops 1073741824 | bytes 8650752 | tf_op jit(solution)/shard_map/hnab,nshbc->nsac/dot_general | solution.py:49
  87.8 75.9 %all-reduce.1 = bf16[1,16,256,256]{2,3,1,0:T(8,128)(2,1)S(1)} all-reduce(f32[1,16,256,256]{2,3,1,0:T(8,128)} %fusion.11), channel_id=1, replica_groups=mesh['bond'=8,'mpo'=4] {'mpo'}, use_global_device_ids=true, to_apply=%region_2.3 | all-reduce | flops 1048576 | bytes 6291456 | tf_op jit(solution)/shard_map/psum | solution.py:54
  163.7 1.1 select_convert_fusion
  164.8 1.0 copy.14
  (3 shorter events, 0.0 us)
Async XLA Ops:
  6.5 75.1 %copy-start = (bf16[2,1,256,256]{3,2,1,0:T(8,128)(2,1)S(1)}, bf16[2,1,256,256]{3,2,1,0:T(8,128)(2,1)}, u32[]{:S(2)}) copy-start(bf16[2,1,256,256]{3,2,1,0:T(8,128)(2,1)} %param.9) | copy-start | bytes 786436
  6.5 3.6 %copy-start.5 = (s32[8]{0:T(128)S(1)}, s32[8]{0:T(128)}, u32[]{:S(2)}) copy-start(s32[8]{0:T(128)} %param.13) | copy-start | bytes 100
  6.5 4.9 %copy-start.2 = (s32[1,16,1]{1,2,0:T(1,128)S(1)}, s32[1,16,1]{1,2,0:T(1,128)}, u32[]{:S(2)}) copy-start(s32[1,16,1]{1,2,0:T(1,128)} %param.12) | copy-start | bytes 196
  6.5 4.9 %copy-start.3 = (s32[8]{0:T(128)S(1)}, s32[8]{0:T(128)}, u32[]{:S(2)}) copy-start(s32[8]{0:T(128)} %param.14) | copy-start | bytes 100
  6.5 4.9 %copy-start.4 = (s32[8]{0:T(128)S(1)}, s32[8]{0:T(128)}, u32[]{:S(2)}) copy-start(s32[8]{0:T(128)} %param.15) | copy-start | bytes 100
  6.5 54.8 %all-gather.2.cloned.1.call-start = ((), (), s32[]{:S(2)}) async-start(), calls=%async_computation | async-start | bytes 2359296 | tf_op jit(solution)/shard_map/all_gather | solution.py:38
  70.4 7.9 %copy-start.1 = (bf16[2,16,16]{2,1,0:T(8,128)(2,1)S(1)}, bf16[2,16,16]{2,1,0:T(8,128)(2,1)}, u32[]{:S(2)}) copy-start(bf16[2,16,16]{2,1,0:T(8,128)(2,1)} %param.11) | copy-start | bytes 3076
Sparse Core Ops, SparseCore 0:
  9.5 51.7 all-gather.1
where the time goes:
time: 173 us
  blocking collectives  75.9 us (44%)
  waiting for transfers between devices  48.3 us (28%)
  local copies, waits for them, and re-layouts  16.7 us (10%)
  matrix products  14.2 us (8%)
  between operations  13.5 us (8%)
  other arithmetic  4.04 us (2%)
    psum x1, blocking collectives, shards(): summed = lax.psum(partial_value, 'mpo')  75.9 us
    all_gather x1, waiting for transfers between devices, shards(): gathered = lax.all_gather(right_environment, 'bond', axis=1, tiled=True)  47.6 us
    dot_general x1, local copies, waits for them, and re-layouts, shards(): jnp.einsum('bac,hbxc->bhax', flat_blocks, chosen, preferred_element_type=...  7.89 us
    dot_general x1, matrix products, shards(): jnp.einsum('hnab,nshbc->nsac', left_environment, mixed, preferred_element...  6.13 us
    dot_general x1, matrix products, shards(): jnp.einsum('bac,hbxc->bhax', flat_blocks, chosen, preferred_element_type=...  4.66 us
    gather x1, local copies, waits for them, and re-layouts, shards(): chosen = jnp.take(gathered, place_flat, axis=1)  4.34 us
  transfers between devices with their start and end apart: 1, of which 1 were waited for; matrix products, arithmetic and copies ran while one was open for 4% of the time, Pallas kernels for 0%

commit v1 on v0

--- a/solution.py
+++ b/solution.py
@@ -2,6 +2,12 @@
 import jax.numpy as jnp
 from jax import lax
 from jax.sharding import PartitionSpec as P
+
+
+def detail_ports(u, on_dim):
+    upper = list(u.shape[1:])
+    upper[on_dim] *= u.shape[0]
+    return jnp.moveaxis(u, 0, on_dim).reshape(upper)
 
 
 def lookup(entries, indices):
@@ -35,7 +41,24 @@
     block_count = sectors * states
     flat_blocks = masked.reshape(block_count, block_rows, block_rows)
     place_flat = lookup(sector_place, sector_ids).reshape(block_count)
-    gathered = lax.all_gather(right_environment, "bond", axis=1, tiled=True)
+    dev_count = lax.psum(1, axis_name="bond")
+    buffer = [(tick, (tick + 1) % dev_count) for tick in range(dev_count)]
+    arr_now, aux = ([], [])
+    crops = [(q, ix) for ix, q in buffer]
+    for at in [*range(dev_count - 1)]:
+        if at % 2 == 0:
+            a_now = lax.ppermute(
+                arr_now[-1] if arr_now else right_environment, axis_name="bond", perm=buffer
+            )
+            arr_now.append(a_now)
+        else:
+            aux.append(
+                lax.ppermute(aux[-1] if aux else right_environment, axis_name="bond", perm=crops)
+            )
+    current_value = jnp.stack([*arr_now[::-1], right_environment, *aux], 0)
+    step_out = lax.axis_index("bond") - len(arr_now)
+    current_value = current_value[(jnp.arange(dev_count) - step_out) % dev_count]
+    gathered = detail_ports(current_value, 1)
     chosen = jnp.take(gathered, place_flat, axis=1)
     right_part = jnp.einsum(
         "bac,hbxc->bhax", flat_blocks, chosen, preferred_element_type=jnp.float32

time: 173 us -> 163 us (0.942)
  waiting for transfers between devices: 48.3 us -> 28.5 us
  starting transfers between devices: 0.04 us -> 15.8 us
  between operations: 13.5 us -> 0.14 us
  local copies, waits for them, and re-layouts: 16.7 us -> 20.6 us
    all_gather x1 -> x0, waiting for transfers between devices: 47.6 us -> none  [shards(): gathered = lax.all_gather(right_environment, 'bond', axis=1, tiled=True)]
    ppermute x0 -> x7, waiting for transfers between devices: none -> 28.5 us  [the longest x4 14.9 us: shards(): lax.ppermute(arr_now[-1] if arr_now else right_environment, axis_name='bo...]
    ppermute x0 -> x7, starting transfers between devices: none -> 15.8 us  [the longest x4 7.97 us: shards(): lax.ppermute(arr_now[-1] if arr_now else right_environment, axis_name='bo...]
    unnamed x13 -> x16, local copies, waits for them, and re-layouts: 2.88 us -> 5.37 us
    gather x0 -> x1, local copies, waits for them, and re-layouts: none -> 2.27 us  [shards(): current_value[(jnp.arange(dev_count) - step_out) % dev_count]]
  transfers between devices with their start and end apart: 1 -> 7, of which waited for: 1 -> 5; matrix products, arithmetic and copies ran while one was open for 4% -> 6% of each run, Pallas kernels for 0% -> 0%
where the time goes in v1:
time: 163 us; the launch traced here: 162 us
  blocking collectives  75.8 us (47%)
  waiting for transfers between devices  28.5 us (17%)
  local copies, waits for them, and re-layouts  20.6 us (13%)
  starting transfers between devices  15.8 us (10%)
  matrix products  15.8 us (10%)
  other arithmetic  5.49 us (3%)
    psum x1, blocking collectives, shards(): summed = lax.psum(partial_value, 'mpo')  75.8 us
    ppermute x4, waiting for transfers between devices, shards(): lax.ppermute(arr_now[-1] if arr_now else right_environment, axis_name='bo...  14.9 us
    ppermute x3, waiting for transfers between devices, shards(): lax.ppermute(aux[-1] if aux else right_environment, axis_name='bond', per...  13.7 us
    ppermute x4, starting transfers between devices, shards(): lax.ppermute(arr_now[-1] if arr_now else right_environment, axis_name='bo...  7.97 us
    dot_general x1, local copies, waits for them, and re-layouts, shards(): jnp.einsum('bac,hbxc->bhax', flat_blocks, chosen, preferred_element_type=...  7.92 us
    ppermute x3, starting transfers between devices, shards(): lax.ppermute(aux[-1] if aux else right_environment, axis_name='bond', per...  7.84 us
    dot_general x1, matrix products, shards(): jnp.einsum('bac,hbxc->bhax', flat_blocks, chosen, preferred_element_type=...  6.24 us
    dot_general x1, matrix products, shards(): jnp.einsum('hnab,nshbc->nsac', left_environment, mixed, preferred_element...  6.13 us
  transfers between devices with their start and end apart: 7, of which 5 were waited for; matrix products, arithmetic and copies ran while one was open for 6% of the time, Pallas kernels for 0%

profile of v1, /device:TPU:0, one launch (start us, length us, event | category | flops | bytes accessed | tf_op | source)
XLA Modules:
  0.0 162.2 jit_solution(12574402560268231379)
XLA Ops:
  0.0 0.0 copy-start
  0.0 3.0 %collective-permute-start = (bf16[2,1,256,256]{3,2,1,0:T(8,128)(2,1)}, bf16[2,1,256,256]{3,2,1,0:T(8,128)(2,1)S(1)}, u32[]{:S(2)}, u32[]{:S(2)}) collective-permute-start(bf16[2,1,256,256]{3,2,1,0:T(8,128)(2,1)} %param.10), channel_id=1, source_target_pairs={{0,4},{4,8},{8,12},{12,16},{16,20},{20,24},{24,28},{28,0},{1,5},{5... | collective-permute-start | bytes 786440 | tf_op jit(solution)/shard_map/ppermute | solution.py:50
  3.0 3.1 %collective-permute-start.4 = (bf16[2,1,256,256]{3,2,0,1:T(8,128)(2,1)}, bf16[2,1,256,256]{3,2,0,1:T(8,128)(2,1)S(1)}, u32[]{:S(2)}, u32[]{:S(2)}) collective-permute-start(bf16[2,1,256,256]{3,2,0,1:T(8,128)(2,1)} %bitcast.69), channel_id=1, source_target_pairs={{4,0},{8,4},{12,8},{16,12},{20,16},{24,20},{28,24},{0,28},{5,1},{9... | collective-permute-start | bytes 786440 | tf_op jit(solution)/shard_map/ppermute | solution.py:56
  6.1 0.8 select_reduce_fusion.1
  6.9 7.6 %collective-permute-done = bf16[2,1,256,256]{3,2,1,0:T(8,128)(2,1)S(1)} collective-permute-done((bf16[2,1,256,256]{3,2,1,0:T(8,128)(2,1)}, bf16[2,1,256,256]{3,2,1,0:T(8,128)(2,1)S(1)}, u32[]{:S(2)}, u32[]{:S(2)}) %collective-permute-start) | collective-permute-done | bytes 262176 | tf_op jit(solution)/shard_map/ppermute | solution.py:50
  14.5 2.4 %collective-permute-start.1 = (bf16[2,1,256,256]{3,2,0,1:T(8,128)(2,1)S(1)}, bf16[2,1,256,256]{3,2,0,1:T(8,128)(2,1)S(1)}, u32[]{:S(2)}, u32[]{:S(2)}) collective-permute-start(bf16[2,1,256,256]{3,2,0,1:T(8,128)(2,1)S(1)} %bitcast.70), channel_id=1, source_target_pairs={{0,4},{4,8},{8,12},{12,16},{16,20},{20,24},{24,28},{28,0},{1,5},{5... | collective-permute-start | bytes 786440 | tf_op jit(solution)/shard_map/ppermute | solution.py:50
  16.9 1.2 dynamic_slice.9
  18.1 0.8 broadcast_compare_fusion
  18.9 6.4 %collective-permute-done.1 = bf16[2,1,256,256]{3,2,0,1:T(8,128)(2,1)S(1)} collective-permute-done((bf16[2,1,256,256]{3,2,0,1:T(8,128)(2,1)S(1)}, bf16[2,1,256,256]{3,2,0,1:T(8,128)(2,1)S(1)}, u32[]{:S(2)}, u32[]{:S(2)}) %collective-permute-start.1) | collective-permute-done | bytes 262176 | tf_op jit(solution)/shard_map/ppermute | solution.py:50
  25.3 0.0 collective-permute-start.2
  25.3 0.7 iota_compare_fusion.2
  26.0 3.9 %copy.16 = bf16[1,16,256,256]{2,3,1,0:T(8,128)(2,1)} copy(bf16[1,16,256,256]{3,2,1,0:T(8,128)(2,1)} %param.8) | data formatting | bytes 4194304 | tf_op args[0]
  29.9 0.0 copy-start.2
  29.9 0.1 iota_compare_fusion
  30.0 0.0 collective-permute-done.4
  30.0 4.7 %collective-permute-start.5 = (bf16[2,1,256,256]{3,2,0,1:T(8,128)(2,1)S(1)}, bf16[2,1,256,256]{3,2,0,1:T(8,128)(2,1)S(1)}, u32[]{:S(2)}, u32[]{:S(2)}) collective-permute-start(bf16[2,1,256,256]{3,2,0,1:T(8,128)(2,1)S(1)} %collective-permute-done.4), channel_id=1, source_target_pairs={{4,0},{8,4},{12,8},{16,12},{20,16},{24,20},{28,24},{0,28},{5,1},{9... | collective-permute-start | bytes 786440 | tf_op jit(solution)/shard_map/ppermute | solution.py:56
  34.7 0.8 collective-permute-done.2
  35.5 2.6 %collective-permute-start.3 = (bf16[2,1,256,256]{3,2,0,1:T(8,128)(2,1)S(1)}, bf16[2,1,256,256]{3,2,0,1:T(8,128)(2,1)S(1)}, u32[]{:S(2)}, u32[]{:S(2)}) collective-permute-start(bf16[2,1,256,256]{3,2,0,1:T(8,128)(2,1)S(1)} %collective-permute-done.2), channel_id=1, source_target_pairs={{0,4},{4,8},{8,12},{12,16},{16,20},{20,24},{24,28},{28,0},{1,5},{5... | collective-permute-start | bytes 786440 | tf_op jit(solution)/shard_map/ppermute | solution.py:50
  38.2 2.0 %broadcast_and_fusion = pred[1,16,256,256]{2,3,1,0:T(8,128)(4,1)} fusion(pred[16,256]{1,0:T(8,128)(4,1)S(1)} %iota_compare_fusion, pred[256]{0:T(512)(128)(4,1)S(1)} %iota_compare_fusion.2), kind=kLoop, calls=%fused_computation.16 | loop fusion | flops 1048576 | bytes 1052928 | tf_op jit(solution)/shard_map/and | solution.py:39
  40.2 5.7 %collective-permute-done.5 = bf16[2,1,256,256]{3,2,0,1:T(8,128)(2,1)S(1)} collective-permute-done((bf16[2,1,256,256]{3,2,0,1:T(8,128)(2,1)S(1)}, bf16[2,1,256,256]{3,2,0,1:T(8,128)(2,1)S(1)}, u32[]{:S(2)}, u32[]{:S(2)}) %collective-permute-start.5) | collective-permute-done | bytes 262176 | tf_op jit(solution)/shard_map/ppermute | solution.py:56
  45.9 0.0 collective-permute-start.6
  45.9 0.0 collective-permute-done.3
  46.0 0.0 copy-done.2
  46.1 8.0 %collective-permute-done.6 = bf16[2,1,256,256]{3,2,0,1:T(8,128)(2,1)S(1)} collective-permute-done((bf16[2,1,256,256]{3,2,0,1:T(8,128)(2,1)S(1)}, bf16[2,1,256,256]{3,2,0,1:T(8,128)(2,1)S(1)}, u32[]{:S(2)}, u32[]{:S(2)}) %collective-permute-start.6) | collective-permute-done | bytes 262176 | tf_op jit(solution)/shard_map/ppermute | solution.py:56
  54.1 0.0 copy-start.1
  54.1 1.3 copy-done.1
  55.5 2.3 %gather_fusion = bf16[8,2,256,256]{3,2,1,0:T(8,128)(2,1)S(1)} fusion(bf16[8,2,256,256]{3,2,1,0:T(8,128)(2,1)} %bitcast.68, s32[1024]{0:T(1024)S(1)} %pad_clamp_fusion.1), kind=kCustom, calls=%fused_computation | custom fusion | bytes 4194336 | tf_op jit(solution)/shard_map/gather | solution.py:60
  57.7 2.8 %gather_fusion.1 = bf16[16,2,256,256]{3,2,1,0:T(8,128)(2,1)} fusion(bf16[2,8,256,256]{3,2,0,1:T(8,128)(2,1)S(1)} %bitcast.67, s32[1024]{0:T(1024)S(1)} %pad_clamp_fusion), kind=kCustom, calls=%fused_computation.1 | custom fusion | bytes 8388672 | tf_op jit(solution)/shard_map/jit(_take)/gather | solution.py:62
  60.5 6.2 %fusion.2 = bf16[16,2,256,256]{3,2,1,0:T(8,128)(2,1)} fusion(bf16[16,2,256,256]{3,2,1,0:T(8,128)(2,1)} %gather_fusion.1, pred[16]{0:T(512)(128)(4,1)S(1)} %compare_and_fusion, bf16[1,16,256,256]{2,3,1,0:T(8,128)(2,1)} %copy.16, pred[16,256]{1,0:T(8,128)(4,1)S(1)} %iota_compare_fusion, pred[256]{0:T(512)(128)(4,1)S(1)} %iota_compare_fusion.2), kind=kOutput, calls=%fused_computation.4 | convolution fusion | flops 1077936128 | bytes 10490128 | tf_op jit(solution)/shard_map/bac,hbxc->bhax/dot_general | solution.py:63
  66.8 0.0 copy-start.3
  66.8 7.9 %copy.20 = bf16[16,2,256,256]{2,0,3,1:T(8,128)(2,1)} copy(bf16[16,2,256,256]{3,2,1,0:T(8,128)(2,1)} %fusion.2) | data formatting | bytes 8388608 | tf_op jit(solution)/shard_map/bac,hbxc->bhax/dot_general | solution.py:63
  74.7 0.0 copy-done.3
  74.7 3.4 %convert_bitcast_fusion = bf16[16,2,256,256]{3,0,2,1:T(8,128)(2,1)S(1)} fusion(bf16[16,2,256,256]{2,0,3,1:T(8,128)(2,1)} %copy.20, bf16[2,16,16]{2,1,0:T(8,128)(2,1)S(1)} %copy-done.3, pred[16,16]{1,0:T(8,128)(4,1)S(1)} %broadcast_compare_fusion), kind=kOutput, calls=%fused_computation.9 | convolution fusion | flops 69206528 | bytes 8389888 | tf_op jit(solution)/shard_map/nhst,nthac->nshac/dot_general | solution.py:69
  78.1 0.0 copy-done
  78.1 6.1 %fusion.11 = f32[1,16,256,256]{2,3,1,0:T(8,128)} fusion(bf16[16,2,256,256]{3,0,2,1:T(8,128)(2,1)S(1)} %convert_bitcast_fusion, bf16[2,1,256,256]{3,2,1,0:T(8,128)(2,1)S(1)} %copy-done), kind=kOutput, calls=%fused_computation.12 | convolution fusion | flops 1073741824 | bytes 8650752 | tf_op jit(solution)/shard_map/hnab,nshbc->nsac/dot_general | solution.py:72
  84.2 75.8 %all-reduce.1 = bf16[1,16,256,256]{2,3,1,0:T(8,128)(2,1)S(1)} all-reduce(f32[1,16,256,256]{2,3,1,0:T(8,128)} %fusion.11), channel_id=1, replica_groups=mesh['bond'=8,'mpo'=4] {'mpo'}, use_global_device_ids=true, to_apply=%region_2.3 | all-reduce | flops 1048576 | bytes 6291456 | tf_op jit(solution)/shard_map/psum | solution.py:77
  160.1 1.1 select_convert_fusion
  161.2 1.0 copy.18
  (13 shorter events, 0.2 us)
Async XLA Ops:
  0.0 78.1 %copy-start = (bf16[2,1,256,256]{3,2,1,0:T(8,128)(2,1)S(1)}, bf16[2,1,256,256]{3,2,1,0:T(8,128)(2,1)}, u32[]{:S(2)}) copy-start(bf16[2,1,256,256]{3,2,1,0:T(8,128)(2,1)} %param.9) | copy-start | bytes 786436
  0.0 14.5 %collective-permute-start = (bf16[2,1,256,256]{3,2,1,0:T(8,128)(2,1)}, bf16[2,1,256,256]{3,2,1,0:T(8,128)(2,1)S(1)}, u32[]{:S(2)}, u32[]{:S(2)}) collective-permute-start(bf16[2,1,256,256]{3,2,1,0:T(8,128)(2,1)} %param.10), channel_id=1, source_target_pairs={{0,4},{4,8},{8,12},{12,16},{16,20},{20,24},{24,28},{28,0},{1,5},{5... | collective-permute-start | bytes 786440 | tf_op jit(solution)/shard_map/ppermute | solution.py:50
  3.0 27.0 %collective-permute-start.4 = (bf16[2,1,256,256]{3,2,0,1:T(8,128)(2,1)}, bf16[2,1,256,256]{3,2,0,1:T(8,128)(2,1)S(1)}, u32[]{:S(2)}, u32[]{:S(2)}) collective-permute-start(bf16[2,1,256,256]{3,2,0,1:T(8,128)(2,1)} %bitcast.69), channel_id=1, source_target_pairs={{4,0},{8,4},{12,8},{16,12},{20,16},{24,20},{28,24},{0,28},{5,1},{9... | collective-permute-start | bytes 786440 | tf_op jit(solution)/shard_map/ppermute | solution.py:56
  14.5 10.9 %collective-permute-start.1 = (bf16[2,1,256,256]{3,2,0,1:T(8,128)(2,1)S(1)}, bf16[2,1,256,256]{3,2,0,1:T(8,128)(2,1)S(1)}, u32[]{:S(2)}, u32[]{:S(2)}) collective-permute-start(bf16[2,1,256,256]{3,2,0,1:T(8,128)(2,1)S(1)} %bitcast.70), channel_id=1, source_target_pairs={{0,4},{4,8},{8,12},{12,16},{16,20},{20,24},{24,28},{28,0},{1,5},{5... | collective-permute-start | bytes 786440 | tf_op jit(solution)/shard_map/ppermute | solution.py:50
  25.3 10.2 %collective-permute-start.2 = (bf16[2,1,256,256]{3,2,0,1:T(8,128)(2,1)S(1)}, bf16[2,1,256,256]{3,2,0,1:T(8,128)(2,1)S(1)}, u32[]{:S(2)}, u32[]{:S(2)}) collective-permute-start(bf16[2,1,256,256]{3,2,0,1:T(8,128)(2,1)S(1)} %collective-permute-done.1), channel_id=1, source_target_pairs={{0,4},{4,8},{8,12},{12,16},{16,20},{20,24},{24,28},{28,0},{1,5},{5... | collective-permute-start | bytes 786440 | tf_op jit(solution)/shard_map/ppermute | solution.py:50
  29.9 16.1 %copy-start.2 = (bf16[2,1,256,256]{3,2,1,0:T(8,128)(2,1)S(1)}, bf16[2,1,256,256]{3,2,1,0:T(8,128)(2,1)}, u32[]{:S(2)}) copy-start(bf16[2,1,256,256]{3,2,1,0:T(8,128)(2,1)} %param.10) | copy-start | bytes 786436
  30.0 15.9 %collective-permute-start.5 = (bf16[2,1,256,256]{3,2,0,1:T(8,128)(2,1)S(1)}, bf16[2,1,256,256]{3,2,0,1:T(8,128)(2,1)S(1)}, u32[]{:S(2)}, u32[]{:S(2)}) collective-permute-start(bf16[2,1,256,256]{3,2,0,1:T(8,128)(2,1)S(1)} %collective-permute-done.4), channel_id=1, source_target_pairs={{4,0},{8,4},{12,8},{16,12},{20,16},{24,20},{28,24},{0,28},{5,1},{9... | collective-permute-start | bytes 786440 | tf_op jit(solution)/shard_map/ppermute | solution.py:56
  35.5 10.3 %collective-permute-start.3 = (bf16[2,1,256,256]{3,2,0,1:T(8,128)(2,1)S(1)}, bf16[2,1,256,256]{3,2,0,1:T(8,128)(2,1)S(1)}, u32[]{:S(2)}, u32[]{:S(2)}) collective-permute-start(bf16[2,1,256,256]{3,2,0,1:T(8,128)(2,1)S(1)} %collective-permute-done.2), channel_id=1, source_target_pairs={{0,4},{4,8},{8,12},{12,16},{16,20},{20,24},{24,28},{28,0},{1,5},{5... | collective-permute-start | bytes 786440 | tf_op jit(solution)/shard_map/ppermute | solution.py:50
  45.9 8.2 %collective-permute-start.6 = (bf16[2,1,256,256]{3,2,0,1:T(8,128)(2,1)S(1)}, bf16[2,1,256,256]{3,2,0,1:T(8,128)(2,1)S(1)}, u32[]{:S(2)}, u32[]{:S(2)}) collective-permute-start(bf16[2,1,256,256]{3,2,0,1:T(8,128)(2,1)S(1)} %collective-permute-done.5), channel_id=1, source_target_pairs={{4,0},{8,4},{12,8},{16,12},{20,16},{24,20},{28,24},{0,28},{5,1},{9... | collective-permute-start | bytes 786440 | tf_op jit(solution)/shard_map/ppermute | solution.py:56
  54.1 1.3 copy-start.1
  66.8 7.9 %copy-start.3 = (bf16[2,16,16]{2,1,0:T(8,128)(2,1)S(1)}, bf16[2,16,16]{2,1,0:T(8,128)(2,1)}, u32[]{:S(2)}) copy-start(bf16[2,16,16]{2,1,0:T(8,128)(2,1)} %param.11) | copy-start | bytes 3076
